TPU v7x, 32 devices: a whole 2x2x4 slice. The times are simulated.
32 devices in a mesh: groups: 2 (over y), wide: 4 (over z), planes: 2 (over x), rep: 2 (over core).
Axes of the slice: x: 2, y: 2, z: 4, core: 2. Of those that a mesh axis runs over, the one named last changes fastest.
Arguments:
- movie_frames: bfloat16 [4, 128, 256, 128], P('planes', ('groups', 'wide'), 'rep'), parts along dimension 1, may hold values from -6 to 6
- pixel_mask: int32 [256, 128], P('rep'), may hold values 0 or 1
- tile_owner: int32 [256, 1], P('rep'), may hold values from 0 to 3; in each aligned block of 128 rows (0 to 127, 128 to 255, ...) at most 48 rows name the same one
- support: int32 [256, 128], P('rep'), may hold values from 0 to 511
- templates: bfloat16 [512, 4, 128], P(None, 'planes'), may hold values from -0.25 to 0.25
- row_taps: float32 [25], replicated, may hold values from -1.25 to 1.25
- col_taps: float32 [25], replicated, may hold values from -1.25 to 1.25
- lag_gains: float32 [4, 3, 65], P('wide'), may hold values from -0.4375 to 0.4375
- dilations: int32 [4, 3], P('wide'), may hold values from 1 to 8
Outputs:
- traces: bfloat16 [128, 128, 256], P('planes', ('groups', 'wide'), 'rep'), parts along dimension 1
- back_projected: bfloat16 [4, 128, 256, 128], P('planes', ('groups', 'wide'), 'rep'), parts along dimension 1
There are 2 independent parts, one for each index of `groups`. A program takes and returns all parts, laid end to end along the dimension named above; an argument that names none is the same for every part. Nothing has to cross between parts.
Inputs may be any that keep to these rules, and one draw needn't show every extreme that they name: Strip h belongs to region class tile_owner[h,0]; the 128 rows of one device name each class at most 48 times.
All inputs are finite; a program needn't handle non-finite values. No bound on the sum of `pixel_mask` on one device may be relied on, other than what follows from the above.
Results may differ from a plain program's by a relative error of at most 0.015.
Values may be sent and summed in bfloat16 or wider, within the bound.
A program may use at most 64 MiB of HBM per device.

v0:
```python
import functools

import jax
import jax.numpy as jnp
from jax import lax
from jax.experimental import pallas as pl
from jax.experimental.pallas import tpu as pltpu
from jax.sharding import PartitionSpec as P

MESH = pl.DeviceIdType.MESH
BF = jnp.bfloat16
F32 = jnp.float32


def extended(cells, axis, dim, width):
    count = lax.axis_size(axis)
    ends = count - 1
    head = lax.slice_in_dim(cells, 0, width, axis=dim)
    tail = lax.slice_in_dim(cells, cells.shape[dim] - width, cells.shape[dim], axis=dim)
    return jnp.concatenate(
        [
            lax.ppermute(tail, axis, [(i, (i + 1) % count) for i in range(ends)]),
            cells,
            lax.ppermute(head, axis, [((i + 1) % count, i) for i in range(ends)]),
        ],
        axis=dim,
    )


def band_matrix(tap_values, rows_in, rows_out, sign, offset):
    inner_idx = jnp.arange(rows_in, dtype=jnp.int32)[:, None]
    outer_idx = jnp.arange(rows_out, dtype=jnp.int32)[None, :]
    where_tap = sign * (inner_idx - outer_idx) + offset
    tap_index = jnp.arange(tap_values.shape[0], dtype=jnp.int32)
    picked_taps = where_tap[:, :, None] == tap_index[None, None, :]
    weights = jnp.where(picked_taps, tap_values[None, None, :], jnp.zeros((), tap_values.dtype))
    return jnp.sum(weights, axis=2).astype(BF)


def lag_matrix(cluster_gains, cluster_lags, frame_count):
    tap_count = cluster_gains.shape[1]
    half_taps = (tap_count - 1) // 2
    lag_values = jnp.arange(2 * frame_count - 1, dtype=jnp.int32) - (frame_count - 1)
    tap_offsets = jnp.arange(tap_count, dtype=jnp.int32) - half_taps
    lag_hits = lag_values[None, :, None] == cluster_lags[:, None, None] * tap_offsets[None, None, :]
    spread = jnp.where(lag_hits, cluster_gains[:, None, :], jnp.zeros((), cluster_gains.dtype))
    kernel = jnp.sum(spread, axis=(0, 2))
    padded = jnp.concatenate([kernel, jnp.zeros((1,), kernel.dtype)])
    tiled = jnp.broadcast_to(padded, (frame_count, 2 * frame_count)).reshape(-1)
    tiled = tiled[: frame_count * (2 * frame_count - 1)].reshape(frame_count, 2 * frame_count - 1)
    return tiled[:, frame_count - 1 :].astype(BF)


def mid_kernel(
    f_ref, sup_ref, own_ref, temp_ref, lag_ref, mask_ref,
    res_ref, tr_ref,
    hot, pall, part, xrecv, zsend, gath, lag_all, tbuf, tr_all, fold,
    lag_s, lag_r, x1_s, x1_r, z1_s, z1_r, z2_s, z2_r, x2_s, x2_r,
):
    np_ = lax.axis_size("planes")
    nw = lax.axis_size("wide")
    p = lax.axis_index("planes")
    z = lax.axis_index("wide")
    blocks, hb, frames, comps = part.shape
    shapes = temp_ref.shape[0]
    tile = min(256, shapes)
    total = nw * frames

    barrier = pltpu.get_barrier_semaphore()
    for k in range(1, nw):
        pl.semaphore_signal(barrier, inc=1, device_id={"wide": lax.rem(z + k, nw)}, device_id_type=MESH)
    for k in range(1, np_):
        pl.semaphore_signal(barrier, inc=1, device_id={"planes": lax.rem(p + k, np_)}, device_id_type=MESH)
    pl.semaphore_wait(barrier, nw - 1 + np_ - 1)

    def to_wide(src, dst, send, recv, k):
        return pltpu.make_async_remote_copy(
            src_ref=src, dst_ref=dst, send_sem=send.at[k - 1], recv_sem=recv.at[k - 1],
            device_id={"wide": lax.rem(z + k, nw)}, device_id_type=MESH)

    def to_plane(src, dst, send, recv, dp, zi):
        slot = (dp - 1) * nw + zi
        return pltpu.make_async_remote_copy(
            src_ref=src, dst_ref=dst, send_sem=send.at[slot], recv_sem=recv.at[slot],
            device_id={"planes": lax.rem(p + dp, np_)}, device_id_type=MESH)

    def lag_copy(k):
        return to_wide(lag_ref, lag_all.at[z], lag_s, lag_r, k)

    def x1_copy(dp, zi):
        return to_plane(part.at[lax.rem(p + dp, np_) * nw + zi], xrecv.at[(dp - 1) * nw + zi], x1_s, x1_r, dp, zi)

    def z1_copy(k):
        return to_wide(zsend.at[lax.rem(z + k, nw)], gath.at[z], z1_s, z1_r, k)

    def z2_copy(k):
        return to_wide(tbuf.at[lax.rem(z + k, nw)], tr_all.at[p * nw + z], z2_s, z2_r, k)

    def x2_copy(dp, zi):
        return to_plane(tr_all.at[p * nw + zi], tr_all.at[p * nw + zi], x2_s, x2_r, dp, zi)

    for k in range(1, nw):
        lag_copy(k).start()
    lag_all[z] = lag_ref[...]

    ids = lax.broadcasted_iota(jnp.int32, (tile, comps), 0)

    def project(b):
        base = b * hb
        f_blk = f_ref[pl.ds(base, hb)].reshape(hb * frames, f_ref.shape[2])
        pall[...] = lax.dot_general(
            f_blk, temp_ref[...], (((1,), (1,)), ((), ())), preferred_element_type=F32).astype(BF)
        sup = sup_ref[b]
        for i in range(hb):
            row = sup[i : i + 1, :]
            for q in range(0, shapes, tile):
                hot[base + i, q : q + tile, :] = jnp.where(ids == row - q, 1.0, 0.0).astype(BF)
            part[b, i] = jnp.dot(
                pall[i * frames : (i + 1) * frames, :], hot[base + i], preferred_element_type=F32).astype(BF)

    def others(n, carry):
        dp = n // nw + 1
        zi = lax.rem(z + 1 + n, nw)
        project(lax.rem(p + dp, np_) * nw + zi)
        x1_copy(dp, zi).start()
        return carry

    lax.fori_loop(0, (np_ - 1) * nw, others, 0)

    def mine(n, carry):
        zi = lax.rem(z + 1 + n, nw)
        b = p * nw + zi
        project(b)
        acc = part[b].astype(F32)
        for dp in range(1, np_):
            x1_copy(dp, zi).wait_recv()
            acc = acc + xrecv[(dp - 1) * nw + zi].astype(F32)
        zsend[zi] = acc.astype(BF)

        @pl.when(n < nw - 1)
        def _():
            z1_copy(n + 1).start()

        return carry

    lax.fori_loop(0, nw, mine, 0)
    gath[z] = zsend[z]

    def arrived(k, carry):
        lag_copy(k).wait()
        z1_copy(k).wait()
        return carry

    lax.fori_loop(1, nw, arrived, 0)

    me = p * nw + z
    for i in range(hb):
        table = lag_all[own_ref[me * hb + i]]
        columns = gath[:, i].reshape(total, comps)
        scores = jnp.dot(table, columns, preferred_element_type=F32)
        tbuf[:, i] = jnp.maximum(scores, 0.0).astype(BF).reshape(nw, frames, comps)

    def give(k, carry):
        z2_copy(k).start()
        return carry

    lax.fori_loop(1, nw, give, 0)
    tr_all[me] = tbuf[z]

    def model(b):
        base = b * hb
        for i in range(hb):
            fold[i * frames : (i + 1) * frames, :] = lax.dot_general(
                tr_all[b, i], hot[base + i], (((1,), (1,)), ((), ())), preferred_element_type=F32).astype(BF)
        out = jnp.dot(fold[...], temp_ref[...], preferred_element_type=F32)
        out = out.reshape(hb, frames, out.shape[1])
        mask = mask_ref[pl.ds(base, hb)]
        res_ref[pl.ds(base, hb)] = (f_ref[pl.ds(base, hb)].astype(F32) - mask * out).astype(BF)

    def same_plane(k, carry):
        zi = lax.rem(z + nw - k, nw)

        @pl.when(k > 0)
        def _():
            z2_copy(lax.max(k, 1)).wait_recv()

        for dp in range(1, np_):
            x2_copy(dp, zi).start()
        model(p * nw + zi)
        return carry

    lax.fori_loop(0, nw, same_plane, 0)

    def other_planes(n, carry):
        dp = n // nw + 1
        zi = lax.rem(z + nw - lax.rem(n, nw), nw)
        x2_copy(dp, zi).wait_recv()
        model(lax.rem(p + np_ - dp, np_) * nw + zi)
        return carry

    lax.fori_loop(0, (np_ - 1) * nw, other_planes, 0)
    tr_ref[...] = tr_all[...]

    def drained_planes(n, carry):
        x1_copy(n // nw + 1, lax.rem(n, nw)).wait_send()
        x2_copy(n // nw + 1, lax.rem(n, nw)).wait_send()
        return carry

    lax.fori_loop(0, (np_ - 1) * nw, drained_planes, 0)

    def drained_wide(k, carry):
        z2_copy(k).wait_send()
        return carry

    lax.fori_loop(1, nw, drained_wide, 0)


def middle(filtered, support, owners, shapes, lag_table, mask):
    np_ = lax.axis_size("planes")
    nw = lax.axis_size("wide")
    blocks = np_ * nw
    rows, frames, pixels = filtered.shape
    hb = rows // blocks
    comps = support.shape[1]
    count = shapes.shape[0]
    total = nw * frames
    vm = pl.BlockSpec(memory_space=pltpu.VMEM)
    dma = pltpu.SemaphoreType.DMA
    piece = (hb, frames, comps)
    res, tr = pl.pallas_call(
        mid_kernel,
        out_shape=(
            jax.ShapeDtypeStruct(filtered.shape, BF),
            jax.ShapeDtypeStruct((blocks,) + piece, BF),
        ),
        in_specs=[vm, vm, pl.BlockSpec(memory_space=pltpu.SMEM), vm, vm, vm],
        out_specs=(vm, vm),
        scratch_shapes=[
            pltpu.VMEM((rows, count, comps), BF),
            pltpu.VMEM((hb * frames, count), BF),
            pltpu.VMEM((blocks,) + piece, BF),
            pltpu.VMEM(((np_ - 1) * nw,) + piece, BF),
            pltpu.VMEM((nw,) + piece, BF),
            pltpu.VMEM((nw,) + piece, BF),
            pltpu.VMEM((nw, total, total), BF),
            pltpu.VMEM((nw,) + piece, BF),
            pltpu.VMEM((blocks,) + piece, BF),
            pltpu.VMEM((hb * frames, count), BF),
            dma((nw - 1,)), dma((nw - 1,)),
            dma(((np_ - 1) * nw,)), dma(((np_ - 1) * nw,)),
            dma((nw - 1,)), dma((nw - 1,)),
            dma((nw - 1,)), dma((nw - 1,)),
            dma(((np_ - 1) * nw,)), dma(((np_ - 1) * nw,)),
        ],
        compiler_params=pltpu.CompilerParams(
            collective_id=0, has_side_effects=True, vmem_limit_bytes=60 * 1024 * 1024
        ),
    )(filtered, support.reshape(blocks, hb, comps), owners, shapes, lag_table, mask)
    return res, tr.reshape(rows, frames, comps)


def on_device(
    movie_frames, pixel_mask, tile_owner, support, templates, row_taps, col_taps, lag_gains, dilations
):
    planes_here, frames_here, rows_here, col_count = movie_frames.shape
    nw = lax.axis_size("wide")
    rim = (row_taps.shape[0] - 1) // 2
    mask_value = pixel_mask.astype(F32)
    col_fwd = band_matrix(col_taps, col_count, col_count, 1, rim)
    smooth = jnp.dot(movie_frames, col_fwd, preferred_element_type=F32).astype(BF)
    padded = extended(smooth, "rep", 2, rim)
    row_fwd = band_matrix(row_taps, rows_here + 2 * rim, rows_here, 1, 0)
    along = jnp.einsum("pfew,eh->hfpw", padded, row_fwd, preferred_element_type=F32)
    filtered = (along * mask_value[:, None, None, :]).astype(BF)
    filtered = filtered.reshape(rows_here, frames_here, planes_here * col_count)
    lag_table = lag_matrix(lag_gains[0], dilations[0], frames_here * nw)
    wide_mask = jnp.tile(mask_value, (1, planes_here))[:, None, :]
    shapes = templates.reshape(templates.shape[0], planes_here * col_count)
    residual, traces = middle(filtered, support, tile_owner[:, 0], shapes, lag_table, wide_mask)

    padded_back = extended(residual, "rep", 0, rim)
    padded_back = padded_back.reshape(rows_here + 2 * rim, frames_here, planes_here, col_count)
    row_adj = band_matrix(row_taps, rows_here + 2 * rim, rows_here, -1, 2 * rim)
    back_rows = jnp.einsum("efpw,eh->pfhw", padded_back, row_adj, preferred_element_type=F32).astype(BF)
    col_adj = band_matrix(col_taps, col_count, col_count, -1, rim)
    back_projected = jnp.dot(back_rows, col_adj, preferred_element_type=F32).astype(BF)

    share = traces.shape[2] // lax.axis_size("planes")
    mine = lax.dynamic_slice_in_dim(traces, lax.axis_index("planes") * share, share, 2)
    return (jnp.transpose(mine, (2, 1, 0)), back_projected)


def solution(mesh):
    return jax.shard_map(
        on_device,
        mesh=mesh,
        in_specs=(
            P("planes", ("groups", "wide"), "rep", None),
            P("rep", None),
            P("rep", None),
            P("rep", None),
            P(None, "planes", None),
            P(),
            P(),
            P("wide", None, None),
            P("wide", None),
        ),
        out_specs=(
            P("planes", ("groups", "wide"), "rep"),
            P("planes", ("groups", "wide"), "rep", None),
        ),
        check_vma=False,
    )
```

profile of v0, /device:TPU:1, one launch (start us, length us, event | category | flops | bytes accessed | tf_op | source)
XLA Modules:
  0.0 60.3 jit_solution(15446643833254131974)
XLA Ops:
  0.6 0.0 copy-start
  0.7 1.7 %select_reduce_fusion.2 = (bf16[128,128]{1,0:T(8,128)(2,1)}, bf16[128,128]{1,0:T(8,128)(2,1)S(1)}) fusion(s32[128,128]{1,0:T(8,128)S(1)} %get-tuple-element.14, f32[25]{0:T(128)} %param.15, s32[128,128]{1,0:T(8,128)S(1)} %get-tuple-element.15), kind=kLoop, calls=%fused_computation.5 | loop fusion | flops 2424832 | bytes 196708 | tf_op jit(solution)/shard_map/reduce_sum | solution.py:37
  2.4 0.0 copy-start.3
  2.4 0.0 copy-start.2
  2.5 0.4 fusion.1
  2.9 1.3 %collective-permute-start = (bf16[2,16,12,128]{3,2,1,0:T(8,128)(2,1)S(1)}, bf16[2,16,12,128]{3,2,1,0:T(8,128)(2,1)S(1)}, u32[]{:S(2)}, u32[]{:S(2)}) collective-permute-start(bf16[2,16,12,128]{3,2,1,0:T(8,128)(2,1)S(1)} %get-tuple-element.12), channel_id=1, source_target_pairs={{0,1},{2,3},{4,5},{6,7},{8,9},{10,11},{12,13},{14,15},{16,17},{18,... | collective-permute-start | bytes 294920 | tf_op jit(solution)/shard_map/ppermute | solution.py:22
  4.2 3.0 %collective-permute-start.1 = (bf16[2,16,12,128]{3,2,1,0:T(8,128)(2,1)S(1)}, bf16[2,16,12,128]{3,2,1,0:T(8,128)(2,1)S(1)}, u32[]{:S(2)}, u32[]{:S(2)}) collective-permute-start(bf16[2,16,12,128]{3,2,1,0:T(8,128)(2,1)S(1)} %get-tuple-element.13), channel_id=1, source_target_pairs={{1,0},{3,2},{5,4},{7,6},{9,8},{11,10},{13,12},{15,14},{17,16},{19,... | collective-permute-start | bytes 294920 | tf_op jit(solution)/shard_map/ppermute | solution.py:24
  7.4 0.1 broadcast_multiply_fusion
  7.4 0.1 select_reduce_fusion.4
  7.6 0.1 maximum_convert_fusion
  7.7 1.1 %select_reduce_fusion = (bf16[152,128]{1,0:T(8,128)(2,1)}, bf16[152,128]{1,0:T(8,128)(2,1)}) fusion(s32[152,128]{1,0:T(8,128)S(1)} %get-tuple-element.16, f32[25]{0:T(128)S(1)} %copy-done.5, s32[152,128]{1,0:T(8,128)S(1)} %get-tuple-element.17), kind=kLoop, calls=%fused_computation.1 | loop fusion | flops 2879488 | bytes 233572 | tf_op jit(solution)/shard_map/reduce_sum | solution.py:37
  8.7 0.1 copy.14
  8.8 0.7 %copy.29 = bf16[64,8,2,128]{3,1,2,0:T(8,128)(2,1)} copy(bf16[64,8,2,128]{3,2,1,0:T(2,128)(2,1)S(1)} %bitcast.48) | data formatting | bytes 524288
  9.6 0.2 reshape.128
  9.7 0.7 %slice.29.lag_ref = bf16[64,64]{1,0:T(8,128)(2,1)} slice(bf16[64,127]{1,0:T(8,128)(2,1)S(1)} %reshape.128), slice={[0:64], [63:127]} | slice | bytes 16384 | tf_op jit(solution)/shard_map/slice | solution.py:51
  10.4 0.0 collective-permute-done
  10.4 0.0 collective-permute-done.1
  10.4 0.6 %copy-done.7 = bf16[2,16,12,128]{3,2,1,0:T(8,128)(2,1)} copy-done((bf16[2,16,12,128]{3,2,1,0:T(8,128)(2,1)}, bf16[2,16,12,128]{3,2,1,0:T(8,128)(2,1)S(1)}, u32[]{:S(2)}) %copy-start.7) | copy-done | bytes 98328
  11.1 0.7 %copy-done.8 = bf16[2,16,12,128]{3,2,1,0:T(8,128)(2,1)} copy-done((bf16[2,16,12,128]{3,2,1,0:T(8,128)(2,1)}, bf16[2,16,12,128]{3,2,1,0:T(8,128)(2,1)S(1)}, u32[]{:S(2)}) %copy-start.8) | copy-done | bytes 98328
  11.7 1.9 %fusion = bf16[128,16,2,128]{0,3,1,2:T(8,128)(2,1)S(1)} fusion(bf16[2,16,12,128]{3,2,1,0:T(8,128)(2,1)} %copy-done.8, bf16[2,16,128,128]{3,2,1,0:T(8,128)(2,1)S(1)} %fusion.1, bf16[2,16,12,128]{3,2,1,0:T(8,128)(2,1)} %copy-done.7, f32[128,128]{0,1:T(8,128)S(1)} %copy.14, bf16[152,128]{1,0:T(8,128)(2,1)} %get-tuple-element.9), kind=kOutput, calls=%fused_computation.12 | convolution fusion | flops 164167680 | bytes 2398208 | tf_op jit(solution)/shard_map/pfew,eh->hfpw/dot_general | solution.py:273
  13.7 1.0 %copy.15 = bf16[128,16,2,128]{3,2,1,0:T(2,128)(2,1)S(1)} copy(bf16[128,16,2,128]{0,3,1,2:T(8,128)(2,1)S(1)} %fusion) | data formatting | bytes 2097152 | tf_op jit(solution)/shard_map/convert_element_type | solution.py:274
  14.7 1.5 %reshape.124.f_ref = bf16[128,16,256]{2,1,0:T(8,128)(2,1)} reshape(bf16[128,16,2,128]{3,2,1,0:T(2,128)(2,1)S(1)} %copy.15) | data formatting | bytes 2097152 | tf_op jit(solution)/shard_map/reshape | solution.py:275
  16.2 0.7 %tile.8 = f32[128,2,128]{2,1,0:T(2,128)} broadcast(f32[128,128]{1,0:T(8,128)S(1)} %convert_element_type.41), dimensions={0,2} | broadcast | bytes 196608 | tf_op jit(solution)/shard_map/tile | solution.py:277
  16.9 28.6 %shard_map.104 = (bf16[128,16,256]{2,1,0:T(8,128)(2,1)}, bf16[8,16,16,128]{3,2,1,0:T(8,128)(2,1)}) custom-call(bf16[128,16,256]{2,1,0:T(8,128)(2,1)} %reshape.124.f_ref, s32[8,16,128]{2,1,0:T(8,128)} %bitcast.49, s32[128]{0:T(128)} %bitcast.52, bf16[512,256]{1,0:T(8,128)(2,1)} %bitcast.44, bf16[64,64]{1,0:T(8,128)(2,1)} %slice.29.lag_ref, ...), custom_call_target="tpu_custom_call" | custom-call | tf_op jit(solution)/shard_map/pallas_call | solution.py:230
  45.5 1.0 %fusion.22 = (bf16[12,16,256]{2,1,0:T(8,128)(2,1)S(1)}, bf16[12,16,256]{2,1,0:T(8,128)(2,1)S(1)}) fusion(bf16[128,16,256]{2,1,0:T(8,128)(2,1)} %get-tuple-element.5), kind=kLoop, calls=%fused_computation.45 | loop fusion | bytes 393216 | tf_op jit(solution)/shard_map/slice | solution.py:19
  46.5 1.3 %collective-permute-start.2 = (bf16[12,16,256]{2,1,0:T(8,128)(2,1)S(1)}, bf16[12,16,256]{2,1,0:T(8,128)(2,1)}, u32[]{:S(2)}, u32[]{:S(2)}) collective-permute-start(bf16[12,16,256]{2,1,0:T(8,128)(2,1)S(1)} %get-tuple-element.10), channel_id=1, source_target_pairs={{0,1},{2,3},{4,5},{6,7},{8,9},{10,11},{12,13},{14,15},{16,17},{18,... | collective-permute-start | bytes 294920 | tf_op jit(solution)/shard_map/ppermute | solution.py:22
  47.8 5.4 %collective-permute-start.3 = (bf16[12,16,256]{2,1,0:T(8,128)(2,1)S(1)}, bf16[12,16,256]{2,1,0:T(8,128)(2,1)}, u32[]{:S(2)}, u32[]{:S(2)}) collective-permute-start(bf16[12,16,256]{2,1,0:T(8,128)(2,1)S(1)} %get-tuple-element.11), channel_id=1, source_target_pairs={{1,0},{3,2},{5,4},{7,6},{9,8},{11,10},{13,12},{15,14},{17,16},{19,... | collective-permute-start | bytes 294920 | tf_op jit(solution)/shard_map/ppermute | solution.py:24
  53.2 1.2 %constant_dynamic-slice_fusion = bf16[128,16,64]{2,1,0:T(8,128)(2,1)S(1)} fusion(bf16[128,16,128]{2,1,0:T(8,128)(2,1)} %bitcast.45, s32[]{:T(128)S(6)} %select_n.24), kind=kLoop, calls=%fused_computation.43 | loop fusion | bytes 524292 | tf_op jit(solution)/shard_map/dynamic_slice | solution.py:289
  54.5 1.3 %copy.22 = bf16[128,16,64]{0,1,2:T(8,128)(2,1)} copy(bf16[128,16,64]{2,1,0:T(8,128)(2,1)S(1)} %constant_dynamic-slice_fusion) | data formatting | bytes 524288
  55.8 1.1 %pad_maximum_fusion = bf16[152,16,256]{2,1,0:T(8,128)(2,1)S(1)} fusion(bf16[12,16,256]{2,1,0:T(8,128)(2,1)} %collective-permute-done.3, bf16[128,16,256]{2,1,0:T(8,128)(2,1)S(1)} %copy-done.1, bf16[12,16,256]{2,1,0:T(8,128)(2,1)} %collective-permute-done.2), kind=kLoop, calls=%fused_computation.20 | loop fusion | flops 1245184 | bytes 2490368 | tf_op jit(solution)/shard_map/concatenate | solution.py:20
  56.9 0.3 reshape.130
  57.2 3.1 %convolution_convert_fusion = bf16[2,16,128,128]{3,2,1,0:T(8,128)(2,1)} fusion(bf16[152,16,2,128]{3,2,1,0:T(2,128)(2,1)S(1)} %reshape.130, bf16[152,128]{1,0:T(8,128)(2,1)} %get-tuple-element.8, bf16[128,128]{1,0:T(8,128)(2,1)} %get-tuple-element.6), kind=kOutput, calls=%fused_computation.9 | convolution fusion | flops 294649856 | bytes 2365440 | tf_op jit(solution)/shard_map/dot_general | solution.py:286
  (23 shorter events, 0.1 us)
Async XLA Ops:
  0.6 1.8 %copy-start = (bf16[2,16,128,128]{3,2,1,0:T(8,128)(2,1)S(1)}, bf16[2,16,128,128]{3,2,1,0:T(8,128)(2,1)}, u32[]{:S(2)}) copy-start(bf16[2,16,128,128]{3,2,1,0:T(8,128)(2,1)} %param.9) | copy-start | bytes 3145732
  2.4 4.9 %copy-start.4 = (f32[1,3,65]{2,0,1:T(1,128)S(1)}, f32[1,3,65]{2,0,1:T(1,128)}, u32[]{:S(2)}) copy-start(f32[1,3,65]{2,0,1:T(1,128)} %param.16) | copy-start | bytes 2344
  2.4 4.9 %copy-start.6 = (s32[1,3]{1,0:T(1,128)S(1)}, s32[1,3]{1,0:T(1,128)}, u32[]{:S(2)}) copy-start(s32[1,3]{1,0:T(1,128)} %param.17) | copy-start | bytes 40
  2.4 5.2 %copy-start.5 = (f32[25]{0:T(128)S(1)}, f32[25]{0:T(128)}, u32[]{:S(2)}) copy-start(f32[25]{0:T(128)} %param.14) | copy-start | bytes 304
  2.4 6.3 %copy-start.3 = (s32[128,128]{1,0:T(8,128)S(1)}, s32[128,128]{1,0:T(8,128)}, u32[]{:S(2)}) copy-start(s32[128,128]{1,0:T(8,128)} %param.10) | copy-start | bytes 196612
  2.4 6.4 %copy-start.2 = (bf16[512,2,128]{2,1,0:T(2,128)(2,1)S(1)}, bf16[512,2,128]{2,1,0:T(2,128)(2,1)}, u32[]{:S(2)}) copy-start(bf16[512,2,128]{2,1,0:T(2,128)(2,1)} %param.13) | copy-start | bytes 786436
  2.9 7.5 %collective-permute-start = (bf16[2,16,12,128]{3,2,1,0:T(8,128)(2,1)S(1)}, bf16[2,16,12,128]{3,2,1,0:T(8,128)(2,1)S(1)}, u32[]{:S(2)}, u32[]{:S(2)}) collective-permute-start(bf16[2,16,12,128]{3,2,1,0:T(8,128)(2,1)S(1)} %get-tuple-element.12), channel_id=1, source_target_pairs={{0,1},{2,3},{4,5},{6,7},{8,9},{10,11},{12,13},{14,15},{16,17},{18,... | collective-permute-start | bytes 294920 | tf_op jit(solution)/shard_map/ppermute | solution.py:22
  4.2 6.2 %collective-permute-start.1 = (bf16[2,16,12,128]{3,2,1,0:T(8,128)(2,1)S(1)}, bf16[2,16,12,128]{3,2,1,0:T(8,128)(2,1)S(1)}, u32[]{:S(2)}, u32[]{:S(2)}) collective-permute-start(bf16[2,16,12,128]{3,2,1,0:T(8,128)(2,1)S(1)} %get-tuple-element.13), channel_id=1, source_target_pairs={{1,0},{3,2},{5,4},{7,6},{9,8},{11,10},{13,12},{15,14},{17,16},{19,... | collective-permute-start | bytes 294920 | tf_op jit(solution)/shard_map/ppermute | solution.py:24
  10.4 0.6 %copy-start.7 = (bf16[2,16,12,128]{3,2,1,0:T(8,128)(2,1)}, bf16[2,16,12,128]{3,2,1,0:T(8,128)(2,1)S(1)}, u32[]{:S(2)}) copy-start(bf16[2,16,12,128]{3,2,1,0:T(8,128)(2,1)S(1)} %collective-permute-done) | copy-start | bytes 294916
  11.1 0.7 %copy-start.8 = (bf16[2,16,12,128]{3,2,1,0:T(8,128)(2,1)}, bf16[2,16,12,128]{3,2,1,0:T(8,128)(2,1)S(1)}, u32[]{:S(2)}) copy-start(bf16[2,16,12,128]{3,2,1,0:T(8,128)(2,1)S(1)} %collective-permute-done.1) | copy-start | bytes 294916
  45.5 10.3 %copy-start.1 = (bf16[128,16,256]{2,1,0:T(8,128)(2,1)S(1)}, bf16[128,16,256]{2,1,0:T(8,128)(2,1)}, u32[]{:S(2)}) copy-start(bf16[128,16,256]{2,1,0:T(8,128)(2,1)} %get-tuple-element.5) | copy-start | bytes 3145732
  46.5 9.2 %collective-permute-start.2 = (bf16[12,16,256]{2,1,0:T(8,128)(2,1)S(1)}, bf16[12,16,256]{2,1,0:T(8,128)(2,1)}, u32[]{:S(2)}, u32[]{:S(2)}) collective-permute-start(bf16[12,16,256]{2,1,0:T(8,128)(2,1)S(1)} %get-tuple-element.10), channel_id=1, source_target_pairs={{0,1},{2,3},{4,5},{6,7},{8,9},{10,11},{12,13},{14,15},{16,17},{18,... | collective-permute-start | bytes 294920 | tf_op jit(solution)/shard_map/ppermute | solution.py:22
  47.8 8.0 %collective-permute-start.3 = (bf16[12,16,256]{2,1,0:T(8,128)(2,1)S(1)}, bf16[12,16,256]{2,1,0:T(8,128)(2,1)}, u32[]{:S(2)}, u32[]{:S(2)}) collective-permute-start(bf16[12,16,256]{2,1,0:T(8,128)(2,1)S(1)} %get-tuple-element.11), channel_id=1, source_target_pairs={{1,0},{3,2},{5,4},{7,6},{9,8},{11,10},{13,12},{15,14},{17,16},{19,... | collective-permute-start | bytes 294920 | tf_op jit(solution)/shard_map/ppermute | solution.py:24
where the time goes:
time: 60.7 us; the launch traced here: 60.3 us
  Pallas kernels  28.6 us (47%)
  starting transfers between devices  11 us (18%)
  local copies, waits for them, and re-layouts  10.1 us (17%)
  matrix products  5.43 us (9%)
  other arithmetic  4.26 us (7%)
  between operations  0.83 us (1%)
    pallas_call x1, Pallas kernels, middle(): pl.pallas_call(mid_kernel, out_shape=(jax.ShapeDtypeStruct(filtered.shape...  28.6 us
    ppermute x2, starting transfers between devices, extended(): lax.ppermute(head, axis, [((i + 1) % count, i) for i in range(ends)])  8.46 us
    unnamed x21, local copies, waits for them, and re-layouts  3.35 us
    dot_general x1, matrix products, on_device(): jnp.dot(back_rows, col_adj, preferred_element_type=F32).astype(BF)  3.07 us
    reduce_sum x2, other arithmetic, band_matrix(): return jnp.sum(weights, axis=2).astype(BF)  2.83 us
    ppermute x2, starting transfers between devices, extended(): lax.ppermute(tail, axis, [(i, (i + 1) % count) for i in range(ends)])  2.58 us
    dot_general x1, matrix products, on_device(): jnp.einsum('pfew,eh->hfpw', padded, row_fwd, preferred_element_type=F32)  1.94 us
    reshape x1, local copies, waits for them, and re-layouts, on_device(): filtered = filtered.reshape(rows_here, frames_here, planes_here * col_count)  1.49 us
  transfers between devices with their start and end apart: 4, of which 0 were waited for; matrix products, arithmetic and copies ran while one was open for 9% of the time, Pallas kernels for 0%

commit v1 on v0

v1 whole, which is shorter than its diff:
```python
import jax
import jax.numpy as jnp
from jax import lax
from jax.experimental import pallas as pl
from jax.experimental.pallas import tpu as pltpu
from jax.sharding import PartitionSpec as P

MESH = pl.DeviceIdType.MESH
BF = jnp.bfloat16
F32 = jnp.float32
I32 = jnp.int32
LANES = 128
TILE = 16


def iota(shape, dim):
    return lax.broadcasted_iota(I32, shape, dim)


def from_taps(tap_ref, where_tap):
    weights = jnp.zeros(where_tap.shape, F32)
    for k in range(tap_ref.shape[0]):
        weights = jnp.where(where_tap == k, tap_ref[k], weights)
    return weights.astype(BF)


def whole_kernel(
    movie_hbm, temp_hbm, sup_ref, mask_ref, own_ref, row_ref, col_ref, gain_ref, dil_ref,
    tr_hbm, back_hbm,
    movie, temp_raw, temp32, temp, temp_t, col_fwd, col_adj, row_fwd, row_adj, lag_own,
    smooth, resid, fbuf, pall, part, xrecv, zsend, gath, lag_all, tbuf, tr_all, tr32, tt32, fold,
    tr_out, back_out,
    in_s, out_s, h1_s, h1_r, h2_s, h2_r,
    lag_s, lag_r, x1_s, x1_r, z1_s, z1_r, z2_s, z2_r, x2_s, x2_r,
):
    np_ = lax.axis_size("planes")
    nw = lax.axis_size("wide")
    nr = lax.axis_size("rep")
    p = lax.axis_index("planes")
    z = lax.axis_index("wide")
    r = lax.axis_index("rep")
    planes, frames, rows, cols = movie.shape
    pixels = planes * cols
    blocks, hb, _, comps = part.shape
    shapes = temp.shape[0]
    total = nw * frames
    pad = (smooth.shape[1] - rows) // 2
    rim = (row_ref.shape[0] - 1) // 2
    col_rim = (col_ref.shape[0] - 1) // 2

    barrier = pltpu.get_barrier_semaphore()
    for k in range(1, nw):
        pl.semaphore_signal(barrier, inc=1, device_id={"wide": lax.rem(z + k, nw)}, device_id_type=MESH)
    for k in range(1, np_):
        pl.semaphore_signal(barrier, inc=1, device_id={"planes": lax.rem(p + k, np_)}, device_id_type=MESH)

    @pl.when(r > 0)
    def _():
        pl.semaphore_signal(barrier, inc=1, device_id={"rep": r - 1}, device_id_type=MESH)

    @pl.when(r < nr - 1)
    def _():
        pl.semaphore_signal(barrier, inc=1, device_id={"rep": r + 1}, device_id_type=MESH)

    movie_in = pltpu.make_async_copy(movie_hbm, movie, in_s.at[0])
    temp_in = pltpu.make_async_copy(temp_hbm, temp_raw, in_s.at[1])
    movie_in.start()
    temp_in.start()

    col_fwd[...] = jnp.zeros(col_fwd.shape, BF)
    col_adj[...] = jnp.zeros(col_adj.shape, BF)
    gap = iota((cols, cols), 0) - iota((cols, cols), 1)
    fwd_block = from_taps(col_ref, gap + col_rim)
    for q in range(planes):
        side = slice(q * cols, (q + 1) * cols)
        col_fwd[side, side] = fwd_block

    zeros = jnp.zeros((frames, pad, pixels), BF)

    @pl.when(r == 0)
    def _():
        smooth[:, :pad, :] = zeros
        resid[:, :pad, :] = zeros

    @pl.when(r == nr - 1)
    def _():
        smooth[:, pad + rows :, :] = zeros
        resid[:, pad + rows :, :] = zeros

    movie_in.wait()
    step = max(1, min(frames, 512 // rows))
    for f in range(0, frames, step):
        x = jnp.concatenate([movie[q, f : f + step].reshape(step * rows, cols) for q in range(planes)], axis=1)
        y = jnp.dot(x, col_fwd[...], preferred_element_type=F32).astype(BF)
        smooth[f : f + step, pad : pad + rows, :] = y.reshape(step, rows, pixels)

    edge = iota((rows, rows + 2 * pad), 1) - iota((rows, rows + 2 * pad), 0) - pad
    row_fwd[...] = from_taps(row_ref, edge + rim)

    taps_t = gain_ref.shape[1]
    wide_lags = 2 * total
    lag = iota((taps_t, wide_lags), 1) - (total - 1)
    offset = iota((taps_t, wide_lags), 0) - (taps_t - 1) // 2
    kern = jnp.zeros((1, wide_lags), F32)
    for b in range(gain_ref.shape[0]):
        hits = jnp.where(lag == dil_ref[b] * offset, 1.0, 0.0)
        kern = kern + jnp.dot(
            gain_ref[b : b + 1, :], hits, precision=lax.Precision.HIGHEST, preferred_element_type=F32)
    kern = jnp.broadcast_to(kern, (TILE, wide_lags))
    for t in range(0, total, TILE):
        turned = pltpu.roll(kern, (total + 1 + t) % wide_lags, 1, stride=1, stride_axis=0)
        lag_own[t : t + TILE, :] = turned[:, :total].astype(BF)

    pl.semaphore_wait(
        barrier, nw - 1 + np_ - 1 + (r > 0).astype(I32) + (r < nr - 1).astype(I32))

    def halo_down(ext, send, recv):
        return pltpu.make_async_remote_copy(
            src_ref=ext.at[:, pl.ds(rows, pad), :], dst_ref=ext.at[:, pl.ds(0, pad), :],
            send_sem=send.at[0], recv_sem=recv.at[0],
            device_id={"rep": lax.rem(r + 1, nr)}, device_id_type=MESH)

    def halo_up(ext, send, recv):
        return pltpu.make_async_remote_copy(
            src_ref=ext.at[:, pl.ds(pad, pad), :], dst_ref=ext.at[:, pl.ds(rows + pad, pad), :],
            send_sem=send.at[1], recv_sem=recv.at[1],
            device_id={"rep": lax.rem(r + nr - 1, nr)}, device_id_type=MESH)

    def halo_start(ext, send, recv):
        @pl.when(r < nr - 1)
        def _():
            halo_down(ext, send, recv).start()

        @pl.when(r > 0)
        def _():
            halo_up(ext, send, recv).start()

    def halo_wait(ext, send, recv):
        @pl.when(r < nr - 1)
        def _():
            halo_down(ext, send, recv).wait_send()
            halo_up(ext, send, recv).wait_recv()

        @pl.when(r > 0)
        def _():
            halo_up(ext, send, recv).wait_send()
            halo_down(ext, send, recv).wait_recv()

    halo_start(smooth, h1_s, h1_r)

    def to_wide(src, dst, send, recv, k):
        return pltpu.make_async_remote_copy(
            src_ref=src, dst_ref=dst, send_sem=send.at[k - 1], recv_sem=recv.at[k - 1],
            device_id={"wide": lax.rem(z + k, nw)}, device_id_type=MESH)

    def to_plane(src, dst, send, recv, dp, zi):
        slot = (dp - 1) * nw + zi
        return pltpu.make_async_remote_copy(
            src_ref=src, dst_ref=dst, send_sem=send.at[slot], recv_sem=recv.at[slot],
            device_id={"planes": lax.rem(p + dp, np_)}, device_id_type=MESH)

    def lag_copy(k):
        return to_wide(lag_own, lag_all.at[z], lag_s, lag_r, k)

    def x1_copy(dp, zi):
        return to_plane(part.at[lax.rem(p + dp, np_) * nw + zi], xrecv.at[(dp - 1) * nw + zi], x1_s, x1_r, dp, zi)

    def z1_copy(k):
        return to_wide(zsend.at[lax.rem(z + k, nw)], gath.at[z], z1_s, z1_r, k)

    def z2_copy(k):
        return to_wide(tbuf.at[lax.rem(z + k, nw)], tr_all.at[p * nw + z], z2_s, z2_r, k)

    def x2_copy(dp, zi):
        return to_plane(tr_all.at[p * nw + zi], tr_all.at[p * nw + zi], x2_s, x2_r, dp, zi)

    for k in range(1, nw):
        lag_copy(k).start()
    lag_all[z] = lag_own[...]

    temp_in.wait()
    temp32[...] = temp_raw[...].astype(F32)
    for q in range(planes):
        side = slice(q * cols, (q + 1) * cols)
        one = temp32[pl.ds(q, shapes, stride=planes), :]
        temp[:, side] = one.astype(BF)
        temp_t[side, :] = jnp.transpose(one).astype(BF)

    mask = mask_ref[...].astype(F32)
    halo_wait(smooth, h1_s, h1_r)
    for f in range(frames):
        along = jnp.dot(row_fwd[...], smooth[f], preferred_element_type=F32)
        for q in range(planes):
            one = along[:, q * cols : (q + 1) * cols] * mask
            fbuf[q, pl.ds(f, rows, stride=frames), :] = one.astype(BF).astype(F32)

    def project(b):
        base = pl.multiple_of(b * hb, hb)
        lines = pl.ds(pl.multiple_of(b * hb * frames, hb * frames), hb * frames)
        x = jnp.concatenate([fbuf[q, lines, :].astype(BF) for q in range(planes)], axis=1)
        pall[...] = jnp.dot(x, temp_t[...], preferred_element_type=F32)
        sup = sup_ref[pl.ds(base, hb), :]
        low = lax.rem(sup, LANES)
        high = lax.div(sup, LANES)
        for i in range(hb):
            lo = jnp.broadcast_to(low[i : i + 1, :], (frames, comps))
            hi = jnp.broadcast_to(high[i : i + 1, :], (frames, comps))
            got = jnp.zeros((frames, comps), F32)
            for q in range(shapes // LANES):
                piece = pall[i * frames : (i + 1) * frames, q * LANES : (q + 1) * LANES]
                picked = jnp.take_along_axis(piece, lo, axis=1, mode="promise_in_bounds")
                got = jnp.where(hi == q, picked, got)
            part[b, i] = got.astype(BF)

    def others(n, carry):
        dp = n // nw + 1
        zi = lax.rem(z + 1 + lax.rem(n, nw), nw)
        project(lax.rem(p + dp, np_) * nw + zi)
        x1_copy(dp, zi).start()
        return carry

    lax.fori_loop(0, (np_ - 1) * nw, others, 0)

    def mine(n, carry):
        zi = lax.rem(z + 1 + n, nw)
        b = p * nw + zi
        project(b)
        acc = part[b].astype(F32)
        for dp in range(1, np_):
            x1_copy(dp, zi).wait_recv()
            acc = acc + xrecv[(dp - 1) * nw + zi].astype(F32)
        zsend[zi] = acc.astype(BF)

        @pl.when(n < nw - 1)
        def _():
            z1_copy(n + 1).start()

        return carry

    lax.fori_loop(0, nw, mine, 0)
    gath[z] = zsend[z]

    row_adj[...] = from_taps(row_ref, rim - edge)
    adj_block = from_taps(col_ref, col_rim - gap)
    for q in range(planes):
        side = slice(q * cols, (q + 1) * cols)
        col_adj[side, side] = adj_block

    def arrived(k, carry):
        lag_copy(k).wait()
        z1_copy(k).wait()
        return carry

    lax.fori_loop(1, nw, arrived, 0)

    me = p * nw + z
    for i in range(hb):
        table = lag_all[own_ref[me * hb + i]]
        columns = gath[:, i].reshape(total, comps)
        scores = jnp.dot(table, columns, preferred_element_type=F32)
        tbuf[:, i] = jnp.maximum(scores, 0.0).astype(BF).reshape(nw, frames, comps)

    def give(k, carry):
        z2_copy(k).start()
        return carry

    lax.fori_loop(1, nw, give, 0)
    tr_all[me] = tbuf[z]

    tile = min(256, shapes)
    groups = tile // TILE
    ids = (iota((groups, TILE, comps), 0) * TILE + iota((groups, TILE, comps), 1)).astype(F32).astype(BF)

    def model(b):
        base = pl.multiple_of(b * hb, hb)
        first = pl.multiple_of(b * hb * frames, hb * frames)
        sup = sup_ref[pl.ds(base, hb), :]
        for i in range(hb):
            now = tr_all[b, i]
            tr32[pl.ds(first + i * frames, frames), :] = now.astype(F32)
            for q in range(0, shapes, tile):
                row = (sup[i : i + 1, :] - q).astype(F32)
                row = jnp.broadcast_to(row, (TILE, comps)).astype(BF)
                hot = jnp.where(ids == row[None], jnp.ones((), BF), jnp.zeros((), BF)).reshape(tile, comps)
                fold[i * frames : (i + 1) * frames, q : q + tile] = lax.dot_general(
                    now, hot, (((1,), (1,)), ((), ())), preferred_element_type=F32).astype(BF)
        out = jnp.dot(fold[...], temp[...], preferred_element_type=F32)
        lines = pl.ds(first, hb * frames)
        for q in range(planes):
            fbuf[q, lines, :] = fbuf[q, lines, :] - out[:, q * cols : (q + 1) * cols]

    def same_plane(k, carry):
        zi = lax.rem(z + nw - k, nw)

        @pl.when(k > 0)
        def _():
            z2_copy(lax.max(k, 1)).wait_recv()

        for dp in range(1, np_):
            x2_copy(dp, zi).start()
        model(p * nw + zi)
        return carry

    lax.fori_loop(0, nw, same_plane, 0)

    def other_planes(n, carry):
        dp = n // nw + 1
        zi = lax.rem(z + nw - lax.rem(n, nw), nw)
        x2_copy(dp, zi).wait_recv()
        model(lax.rem(p + np_ - dp, np_) * nw + zi)
        return carry

    lax.fori_loop(0, (np_ - 1) * nw, other_planes, 0)

    for f in range(frames):
        for q in range(planes):
            one = fbuf[q, pl.ds(f, rows, stride=frames), :] * mask
            resid[f, pad : pad + rows, q * cols : (q + 1) * cols] = one.astype(BF)
    halo_start(resid, h2_s, h2_r)

    share = tr_out.shape[0]
    chosen = iota((share, comps), 1) == iota((share, comps), 0) + p * share
    chosen = jnp.where(chosen, 1.0, 0.0).astype(BF)
    for f in range(frames):
        one = tr32[pl.ds(f, rows, stride=frames), :].astype(BF)
        tt32[pl.ds(f, share, stride=frames), :] = lax.dot_general(
            chosen, one, (((1,), (1,)), ((), ())), preferred_element_type=F32)
    tr_out[...] = tt32[...].astype(BF).reshape(share, frames, rows)
    tr_copy = pltpu.make_async_copy(tr_out, tr_hbm, out_s.at[0])
    tr_copy.start()

    halo_wait(resid, h2_s, h2_r)
    step = max(1, frames // 4)
    copies = []
    for f0 in range(0, frames, step):
        for f in range(f0, f0 + step):
            y = jnp.dot(row_adj[...], resid[f], preferred_element_type=F32).astype(BF)
            y = jnp.dot(y, col_adj[...], preferred_element_type=F32).astype(BF)
            for q in range(planes):
                back_out[q, f] = y[:, q * cols : (q + 1) * cols]
        copy = pltpu.make_async_copy(
            back_out.at[:, pl.ds(f0, step)], back_hbm.at[:, pl.ds(f0, step)], out_s.at[1 + f0 // step])
        copy.start()
        copies.append(copy)

    def drained_planes(n, carry):
        x1_copy(n // nw + 1, lax.rem(n, nw)).wait_send()
        x2_copy(n // nw + 1, lax.rem(n, nw)).wait_send()
        return carry

    lax.fori_loop(0, (np_ - 1) * nw, drained_planes, 0)

    def drained_wide(k, carry):
        z2_copy(k).wait_send()
        return carry

    lax.fori_loop(1, nw, drained_wide, 0)
    tr_copy.wait()
    for copy in copies:
        copy.wait()


def on_device(
    movie_frames, pixel_mask, tile_owner, support, templates, row_taps, col_taps, lag_gains, dilations
):
    planes, frames, rows, cols = movie_frames.shape
    np_ = lax.axis_size("planes")
    nw = lax.axis_size("wide")
    blocks = np_ * nw
    hb = rows // blocks
    comps = support.shape[1]
    shapes = templates.shape[0]
    total = nw * frames
    pixels = planes * cols
    rim = (row_taps.shape[0] - 1) // 2
    pad = -(-rim // TILE) * TILE
    share = comps // np_
    piece = (hb, frames, comps)
    hbm = pl.BlockSpec(memory_space=pl.ANY)
    vm = pl.BlockSpec(memory_space=pltpu.VMEM)
    sm = pl.BlockSpec(memory_space=pltpu.SMEM)
    dma = pltpu.SemaphoreType.DMA
    traces, back = pl.pallas_call(
        whole_kernel,
        out_shape=(
            jax.ShapeDtypeStruct((share, frames, rows), BF),
            jax.ShapeDtypeStruct(movie_frames.shape, BF),
        ),
        in_specs=[hbm, hbm, vm, vm, sm, sm, sm, vm, sm],
        out_specs=(hbm, hbm),
        scratch_shapes=[
            pltpu.VMEM(movie_frames.shape, BF),
            pltpu.VMEM((shapes * planes, cols), BF),
            pltpu.VMEM((shapes * planes, cols), F32),
            pltpu.VMEM((shapes, pixels), BF),
            pltpu.VMEM((pixels, shapes), BF),
            pltpu.VMEM((pixels, pixels), BF),
            pltpu.VMEM((pixels, pixels), BF),
            pltpu.VMEM((rows, rows + 2 * pad), BF),
            pltpu.VMEM((rows, rows + 2 * pad), BF),
            pltpu.VMEM((total, total), BF),
            pltpu.VMEM((frames, rows + 2 * pad, pixels), BF),
            pltpu.VMEM((frames, rows + 2 * pad, pixels), BF),
            pltpu.VMEM((planes, rows * frames, cols), F32),
            pltpu.VMEM((hb * frames, shapes), F32),
            pltpu.VMEM((blocks,) + piece, BF),
            pltpu.VMEM(((np_ - 1) * nw,) + piece, BF),
            pltpu.VMEM((nw,) + piece, BF),
            pltpu.VMEM((nw,) + piece, BF),
            pltpu.VMEM((nw, total, total), BF),
            pltpu.VMEM((nw,) + piece, BF),
            pltpu.VMEM((blocks,) + piece, BF),
            pltpu.VMEM((rows * frames, comps), F32),
            pltpu.VMEM((share * frames, rows), F32),
            pltpu.VMEM((hb * frames, shapes), BF),
            pltpu.VMEM((share, frames, rows), BF),
            pltpu.VMEM(movie_frames.shape, BF),
            dma((2,)), dma((5,)), dma((2,)), dma((2,)), dma((2,)), dma((2,)),
            dma((nw - 1,)), dma((nw - 1,)),
            dma(((np_ - 1) * nw,)), dma(((np_ - 1) * nw,)),
            dma((nw - 1,)), dma((nw - 1,)),
            dma((nw - 1,)), dma((nw - 1,)),
            dma(((np_ - 1) * nw,)), dma(((np_ - 1) * nw,)),
        ],
        compiler_params=pltpu.CompilerParams(
            collective_id=0, has_side_effects=True, vmem_limit_bytes=60 * 1024 * 1024
        ),
    )(
        movie_frames, templates.reshape(shapes * planes, cols), support, pixel_mask, tile_owner[:, 0],
        row_taps, col_taps, lag_gains[0], dilations[0],
    )
    return traces, back


def solution(mesh):
    return jax.shard_map(
        on_device,
        mesh=mesh,
        in_specs=(
            P("planes", ("groups", "wide"), "rep", None),
            P("rep", None),
            P("rep", None),
            P("rep", None),
            P(None, "planes", None),
            P(),
            P(),
            P("wide", None, None),
            P("wide", None),
        ),
        out_specs=(
            P("planes", ("groups", "wide"), "rep"),
            P("planes", ("groups", "wide"), "rep", None),
        ),
        check_vma=False,
    )
```

time: 60.7 us -> 40.9 us (0.67)
  starting transfers between devices: 11 us -> 0 us
  Pallas kernels: 28.6 us -> 34.6 us
  matrix products: 5.43 us -> 0 us
  local copies, waits for them, and re-layouts: 10.1 us -> 5.23 us
  other arithmetic: 4.26 us -> 0 us
    ppermute x4 -> x0, starting transfers between devices: 11 us -> none  [the longest x2 8.46 us: extended(): lax.ppermute(head, axis, [((i + 1) % count, i) for i in range(ends)])]
    pallas_call x1, Pallas kernels: 28.6 us -> 34.6 us  [on_device(): pl.pallas_call(whole_kernel, out_shape=(jax.ShapeDtypeStruct((share, fram...]
    dot_general x3 -> x0, matrix products: 5.43 us -> none  [the longest x1 3.07 us: on_device(): jnp.dot(back_rows, col_adj, preferred_element_type=F32).astype(BF)]
    reduce_sum x3 -> x0, other arithmetic: 2.97 us -> none  [the longest x2 2.83 us: band_matrix(): return jnp.sum(weights, axis=2).astype(BF)]
    reshape x4 -> x0, local copies, waits for them, and re-layouts: 1.98 us -> none  [the longest x1 1.49 us: on_device(): filtered = filtered.reshape(rows_here, frames_here, planes_here * col_count)]
    unnamed x21 -> x5, local copies, waits for them, and re-layouts: 3.35 us -> 5.23 us
    slice x3 -> x0, local copies, waits for them, and re-layouts: 1.77 us -> none  [the longest x2 1.08 us: extended(): lax.slice_in_dim(cells, cells.shape[dim] - width, cells.shape[dim], axis=...]
    dynamic_slice x1 -> x0, local copies, waits for them, and re-layouts: 1.25 us -> none  [on_device(): lax.dynamic_slice_in_dim(traces, lax.axis_index('planes') * share, share, 2)]
  transfers between devices with their start and end apart: 4 -> 0, of which waited for: 0 -> 0; matrix products, arithmetic and copies ran while one was open for 9% -> 0% of each run, Pallas kernels for 0% -> 0%
where the time goes in v1:
time: 40.9 us; the launch traced here: 40.5 us
  Pallas kernels  34.6 us (85%)
  local copies, waits for them, and re-layouts  5.23 us (13%)
  between operations  0.65 us (2%)
    pallas_call x1, Pallas kernels, on_device(): pl.pallas_call(whole_kernel, out_shape=(jax.ShapeDtypeStruct((share, fram...  34.6 us
    unnamed x5, local copies, waits for them, and re-layouts  5.23 us

profile of v1, /device:TPU:1, one launch (start us, length us, event | category | flops | bytes accessed | tf_op | source)
XLA Modules:
  0.0 40.5 jit_solution(1132866997413534059)
XLA Ops:
  0.6 0.0 copy-start
  0.6 0.7 %copy-done = f32[1,3,65]{2,0,1:T(1,128)S(1)} copy-done((f32[1,3,65]{2,0,1:T(1,128)S(1)}, f32[1,3,65]{2,0,1:T(1,128)}, u32[]{:S(2)}) %copy-start) | copy-done | bytes 804
  1.3 0.6 %copy.13 = f32[1,3,65]{2,1,0:T(4,128)} copy(f32[1,3,65]{2,0,1:T(1,128)S(1)} %copy-done) | data formatting | bytes 1560
  1.9 34.6 %shard_map.104 = (bf16[64,16,128]{2,1,0:T(8,128)(2,1)}, bf16[2,16,128,128]{3,2,1,0:T(8,128)(2,1)}) custom-call(bf16[2,16,128,128]{3,2,1,0:T(8,128)(2,1)} %movie_hbm.1, bf16[1024,128]{1,0:T(8,128)(2,1)} %bitcast.6, s32[128,128]{1,0:T(8,128)} %sup_ref.1, s32[128,128]{1,0:T(8,128)} %mask_ref.1, s32[128]{0:T(128)} %bitcast.8, f32[25]{0:T(128)} %row_ref.1, ...), custom_call_target="tpu_custom_call" | custom-call | tf_op jit(solution)/shard_map/pallas_call | solution.py:383
  36.5 1.7 %copy.16 = bf16[64,16,128]{2,1,0:T(8,128)(2,1)} copy(bf16[64,16,128]{2,1,0:T(8,128)(2,1)} %get-tuple-element.4) | data formatting | bytes 524288
  38.2 2.3 %copy.17 = bf16[2,16,128,128]{3,2,1,0:T(8,128)(2,1)} copy(bf16[2,16,128,128]{3,2,1,0:T(8,128)(2,1)} %get-tuple-element.5) | data formatting | bytes 2097152
Async XLA Ops:
  0.6 0.7 %copy-start = (f32[1,3,65]{2,0,1:T(1,128)S(1)}, f32[1,3,65]{2,0,1:T(1,128)}, u32[]{:S(2)}) copy-start(f32[1,3,65]{2,0,1:T(1,128)} %param.16) | copy-start | bytes 2344

commit v2 on v1

--- a/solution.py
+++ b/solution.py
@@ -25,12 +25,11 @@
 
 
 def whole_kernel(
-    movie_hbm, temp_hbm, sup_ref, mask_ref, own_ref, row_ref, col_ref, gain_ref, dil_ref,
-    tr_hbm, back_hbm,
-    movie, temp_raw, temp32, temp, temp_t, col_fwd, col_adj, row_fwd, row_adj, lag_own,
-    smooth, resid, fbuf, pall, part, xrecv, zsend, gath, lag_all, tbuf, tr_all, tr32, tt32, fold,
-    tr_out, back_out,
-    in_s, out_s, h1_s, h1_r, h2_s, h2_r,
+    movie_hbm, temp_hbm, sup_hbm, mask_hbm, own_hbm, row_hbm, col_hbm, gain_hbm, dil_hbm,
+    tr_out, resid, row_adj, col_adj,
+    movie, temp_raw, sup_ref, mask_ref, own_ref, row_ref, col_ref, gain_ref, dil_ref, temp32, temp, temp_t, col_fwd, row_fwd, lag_own,
+    smooth, fbuf, pall, part, xrecv, zsend, gath, lag_all, tbuf, tr_all, tr32, tt32, fold,
+    in_s, h1_s, h1_r, h2_s, h2_r,
     lag_s, lag_r, x1_s, x1_r, z1_s, z1_r, z2_s, z2_r, x2_s, x2_r,
 ):
     np_ = lax.axis_size("planes")
@@ -62,14 +61,17 @@
     def _():
         pl.semaphore_signal(barrier, inc=1, device_id={"rep": r + 1}, device_id_type=MESH)
 
-    movie_in = pltpu.make_async_copy(movie_hbm, movie, in_s.at[0])
-    temp_in = pltpu.make_async_copy(temp_hbm, temp_raw, in_s.at[1])
-    movie_in.start()
-    temp_in.start()
+    col_in, movie_in, row_in, gain_in, dil_in, temp_in, mask_in, sup_in, own_in = [
+        pltpu.make_async_copy(src, dst, in_s.at[n]) for n, (src, dst) in enumerate((
+            (col_hbm, col_ref), (movie_hbm, movie), (row_hbm, row_ref), (gain_hbm, gain_ref), (dil_hbm, dil_ref),
+            (temp_hbm, temp_raw), (mask_hbm, mask_ref), (sup_hbm, sup_ref), (own_hbm, own_ref)))]
+    for copy in (col_in, movie_in, row_in, gain_in, dil_in, temp_in, mask_in, sup_in, own_in):
+        copy.start()
 
     col_fwd[...] = jnp.zeros(col_fwd.shape, BF)
     col_adj[...] = jnp.zeros(col_adj.shape, BF)
     gap = iota((cols, cols), 0) - iota((cols, cols), 1)
+    col_in.wait()
     fwd_block = from_taps(col_ref, gap + col_rim)
     for q in range(planes):
         side = slice(q * cols, (q + 1) * cols)
@@ -95,9 +97,12 @@
         smooth[f : f + step, pad : pad + rows, :] = y.reshape(step, rows, pixels)
 
     edge = iota((rows, rows + 2 * pad), 1) - iota((rows, rows + 2 * pad), 0) - pad
+    row_in.wait()
     row_fwd[...] = from_taps(row_ref, edge + rim)
 
-    taps_t = gain_ref.shape[1]
+    gain_in.wait()
+    dil_in.wait()
+    taps_t = gain_ref.shape[2]
     wide_lags = 2 * total
     lag = iota((taps_t, wide_lags), 1) - (total - 1)
     offset = iota((taps_t, wide_lags), 0) - (taps_t - 1) // 2
@@ -105,7 +110,7 @@
     for b in range(gain_ref.shape[0]):
         hits = jnp.where(lag == dil_ref[b] * offset, 1.0, 0.0)
         kern = kern + jnp.dot(
-            gain_ref[b : b + 1, :], hits, precision=lax.Precision.HIGHEST, preferred_element_type=F32)
+            gain_ref[b], hits, precision=lax.Precision.HIGHEST, preferred_element_type=F32)
     kern = jnp.broadcast_to(kern, (TILE, wide_lags))
     for t in range(0, total, TILE):
         turned = pltpu.roll(kern, (total + 1 + t) % wide_lags, 1, stride=1, stride_axis=0)
@@ -186,6 +191,8 @@
         temp[:, side] = one.astype(BF)
         temp_t[side, :] = jnp.transpose(one).astype(BF)
 
+    for copy in (mask_in, sup_in, own_in):
+        copy.wait()
     mask = mask_ref[...].astype(F32)
     halo_wait(smooth, h1_s, h1_r)
     for f in range(frames):
@@ -326,10 +333,27 @@
         tt32[pl.ds(f, share, stride=frames), :] = lax.dot_general(
             chosen, one, (((1,), (1,)), ((), ())), preferred_element_type=F32)
     tr_out[...] = tt32[...].astype(BF).reshape(share, frames, rows)
-    tr_copy = pltpu.make_async_copy(tr_out, tr_hbm, out_s.at[0])
+
+    halo_wait(resid, h2_s, h2_r)
+
+    def drained_planes(n, carry):
+        x1_copy(n // nw + 1, lax.rem(n, nw)).wait_send()
+        x2_copy(n // nw + 1, lax.rem(n, nw)).wait_send()
+        return carry
+
+    lax.fori_loop(0, (np_ - 1) * nw, drained_planes, 0)
+
+    def drained_wide(k, carry):
+        z2_copy(k).wait_send()
+        return carry
+
+    lax.fori_loop(1, nw, drained_wide, 0)
+
+
+def back_kernel(tr_ref, resid, row_adj, col_adj, tr_hbm, back_hbm, back_out, out_s):
+    planes, frames, rows, cols = back_out.shape
+    tr_copy = pltpu.make_async_copy(tr_ref, tr_hbm, out_s.at[0])
     tr_copy.start()
-
-    halo_wait(resid, h2_s, h2_r)
     step = max(1, frames // 4)
     copies = []
     for f0 in range(0, frames, step):
@@ -342,19 +366,6 @@
             back_out.at[:, pl.ds(f0, step)], back_hbm.at[:, pl.ds(f0, step)], out_s.at[1 + f0 // step])
         copy.start()
         copies.append(copy)
-
-    def drained_planes(n, carry):
-        x1_copy(n // nw + 1, lax.rem(n, nw)).wait_send()
-        x2_copy(n // nw + 1, lax.rem(n, nw)).wait_send()
-        return carry
-
-    lax.fori_loop(0, (np_ - 1) * nw, drained_planes, 0)
-
-    def drained_wide(k, carry):
-        z2_copy(k).wait_send()
-        return carry
-
-    lax.fori_loop(1, nw, drained_wide, 0)
     tr_copy.wait()
     for copy in copies:
         copy.wait()
@@ -376,30 +387,35 @@
     pad = -(-rim // TILE) * TILE
     share = comps // np_
     piece = (hb, frames, comps)
-    hbm = pl.BlockSpec(memory_space=pl.ANY)
+    hbm = pl.BlockSpec(memory_space=pltpu.HBM)
     vm = pl.BlockSpec(memory_space=pltpu.VMEM)
-    sm = pl.BlockSpec(memory_space=pltpu.SMEM)
     dma = pltpu.SemaphoreType.DMA
-    traces, back = pl.pallas_call(
+    middle = pl.pallas_call(
         whole_kernel,
         out_shape=(
             jax.ShapeDtypeStruct((share, frames, rows), BF),
-            jax.ShapeDtypeStruct(movie_frames.shape, BF),
+            jax.ShapeDtypeStruct((frames, rows + 2 * pad, pixels), BF),
+            jax.ShapeDtypeStruct((rows, rows + 2 * pad), BF),
+            jax.ShapeDtypeStruct((pixels, pixels), BF),
         ),
-        in_specs=[hbm, hbm, vm, vm, sm, sm, sm, vm, sm],
-        out_specs=(hbm, hbm),
+        in_specs=[hbm] * 9,
+        out_specs=(vm,) * 4,
         scratch_shapes=[
             pltpu.VMEM(movie_frames.shape, BF),
             pltpu.VMEM((shapes * planes, cols), BF),
+            pltpu.VMEM(support.shape, I32),
+            pltpu.VMEM(pixel_mask.shape, I32),
+            pltpu.SMEM((rows,), I32),
+            pltpu.SMEM(row_taps.shape, F32),
+            pltpu.SMEM(col_taps.shape, F32),
+            pltpu.VMEM((lag_gains.shape[1], 1, lag_gains.shape[2]), F32),
+            pltpu.SMEM((dilations.shape[1],), I32),
             pltpu.VMEM((shapes * planes, cols), F32),
             pltpu.VMEM((shapes, pixels), BF),
             pltpu.VMEM((pixels, shapes), BF),
             pltpu.VMEM((pixels, pixels), BF),
-            pltpu.VMEM((pixels, pixels), BF),
-            pltpu.VMEM((rows, rows + 2 * pad), BF),
             pltpu.VMEM((rows, rows + 2 * pad), BF),
             pltpu.VMEM((total, total), BF),
-            pltpu.VMEM((frames, rows + 2 * pad, pixels), BF),
             pltpu.VMEM((frames, rows + 2 * pad, pixels), BF),
             pltpu.VMEM((planes, rows * frames, cols), F32),
             pltpu.VMEM((hb * frames, shapes), F32),
@@ -413,9 +429,7 @@
             pltpu.VMEM((rows * frames, comps), F32),
             pltpu.VMEM((share * frames, rows), F32),
             pltpu.VMEM((hb * frames, shapes), BF),
-            pltpu.VMEM((share, frames, rows), BF),
-            pltpu.VMEM(movie_frames.shape, BF),
-            dma((2,)), dma((5,)), dma((2,)), dma((2,)), dma((2,)), dma((2,)),
+            dma((9,)), dma((2,)), dma((2,)), dma((2,)), dma((2,)),
             dma((nw - 1,)), dma((nw - 1,)),
             dma(((np_ - 1) * nw,)), dma(((np_ - 1) * nw,)),
             dma((nw - 1,)), dma((nw - 1,)),
@@ -423,13 +437,23 @@
             dma(((np_ - 1) * nw,)), dma(((np_ - 1) * nw,)),
         ],
         compiler_params=pltpu.CompilerParams(
-            collective_id=0, has_side_effects=True, vmem_limit_bytes=60 * 1024 * 1024
+            collective_id=0, has_side_effects=True, vmem_limit_bytes=40 * 1024 * 1024
         ),
-    )(
+    )(*[pltpu.with_memory_space_constraint(x, pltpu.HBM) for x in (
         movie_frames, templates.reshape(shapes * planes, cols), support, pixel_mask, tile_owner[:, 0],
-        row_taps, col_taps, lag_gains[0], dilations[0],
-    )
-    return traces, back
+        row_taps, col_taps, jnp.transpose(lag_gains, (1, 0, 2)), dilations[0],
+    )])
+    return pl.pallas_call(
+        back_kernel,
+        out_shape=(
+            jax.ShapeDtypeStruct((share, frames, rows), BF),
+            jax.ShapeDtypeStruct(movie_frames.shape, BF),
+        ),
+        in_specs=[vm] * 4,
+        out_specs=(hbm, hbm),
+        scratch_shapes=[pltpu.VMEM(movie_frames.shape, BF), dma((5,))],
+        compiler_params=pltpu.CompilerParams(vmem_limit_bytes=16 * 1024 * 1024),
+    )(*middle)
 
 
 def solution(mesh):

time: 40.9 us -> 35 us (0.86)
  local copies, waits for them, and re-layouts: 5.23 us -> 0 us
  Pallas kernels: 34.6 us -> 34.1 us
    unnamed x5 -> x0, local copies, waits for them, and re-layouts: 5.23 us -> none
    pallas_call x1, Pallas kernels: 34.6 us -> 32.5 us  [on_device(): pl.pallas_call(whole_kernel, out_shape=(jax.ShapeDtypeStruct((share, fram...]
    pallas_call x0 -> x1, Pallas kernels: none -> 1.55 us  [on_device(): pl.pallas_call(back_kernel, out_shape=(jax.ShapeDtypeStruct((share, frame...]
where the time goes in v2:
time: 35 us; the launch traced here: 34.7 us
  Pallas kernels  34.1 us (97%)
  between operations  0.64 us (2%)
    pallas_call x1, Pallas kernels, on_device(): pl.pallas_call(whole_kernel, out_shape=(jax.ShapeDtypeStruct((share, fram...  32.5 us
    pallas_call x1, Pallas kernels, on_device(): pl.pallas_call(back_kernel, out_shape=(jax.ShapeDtypeStruct((share, frame...  1.55 us

profile of v2, /device:TPU:1, one launch (start us, length us, event | category | flops | bytes accessed | tf_op | source)
XLA Modules:
  0.0 34.7 jit_solution(17371351158368685914)
XLA Ops:
  0.6 32.5 %shard_map.104 = (bf16[64,16,128]{2,1,0:T(8,128)(2,1)S(1)}, bf16[16,160,256]{2,1,0:T(8,128)(2,1)S(1)}, bf16[128,160]{1,0:T(8,128)(2,1)S(1)}, bf16[256,256]{1,0:T(8,128)(2,1)S(1)}) custom-call(bf16[2,16,128,128]{3,2,1,0:T(8,128)(2,1)} %movie_hbm.1, bf16[1024,128]{1,0:T(8,128)(2,1)} %bitcast.4, s32[128,128]{1,0:T(8,128)} %sup_hbm.1, s32[128,128]{1,0:T(8,128)} %mask_hbm.1, ...), custom_call_target="tpu_custom_call" | custom-call | tf_op jit(solution)/shard_map/pallas_call | solution.py:393
  33.2 1.5 %shard_map.105 = (bf16[64,16,128]{2,1,0:T(8,128)(2,1)}, bf16[2,16,128,128]{3,2,1,0:T(8,128)(2,1)}) custom-call(bf16[64,16,128]{2,1,0:T(8,128)(2,1)S(1)} %get-tuple-element.6.tr_ref, bf16[16,160,256]{2,1,0:T(8,128)(2,1)S(1)} %get-tuple-element.7.resid, bf16[128,160]{1,0:T(8,128)(2,1)S(1)} %get-tuple-element.8.row_adj, ...), custom_call_target="tpu_custom_call" | custom-call | tf_op jit(solution)/shard_map/pallas_call | solution.py:446

commit v3 on v2

--- a/solution.py
+++ b/solution.py
@@ -29,7 +29,7 @@
     tr_out, resid, row_adj, col_adj,
     movie, temp_raw, sup_ref, mask_ref, own_ref, row_ref, col_ref, gain_ref, dil_ref, temp32, temp, temp_t, col_fwd, row_fwd, lag_own,
     smooth, fbuf, pall, part, xrecv, zsend, gath, lag_all, tbuf, tr_all, tr32, tt32, fold,
-    in_s, h1_s, h1_r, h2_s, h2_r,
+    in_s, far_s, h1_s, h1_r, h2_s, h2_r,
     lag_s, lag_r, x1_s, x1_r, z1_s, z1_r, z2_s, z2_r, x2_s, x2_r,
 ):
     np_ = lax.axis_size("planes")
@@ -48,18 +48,20 @@
     col_rim = (col_ref.shape[0] - 1) // 2
 
     barrier = pltpu.get_barrier_semaphore()
-    for k in range(1, nw):
-        pl.semaphore_signal(barrier, inc=1, device_id={"wide": lax.rem(z + k, nw)}, device_id_type=MESH)
     for k in range(1, np_):
         pl.semaphore_signal(barrier, inc=1, device_id={"planes": lax.rem(p + k, np_)}, device_id_type=MESH)
 
-    @pl.when(r > 0)
-    def _():
-        pl.semaphore_signal(barrier, inc=1, device_id={"rep": r - 1}, device_id_type=MESH)
-
-    @pl.when(r < nr - 1)
-    def _():
-        pl.semaphore_signal(barrier, inc=1, device_id={"rep": r + 1}, device_id_type=MESH)
+    def greet(sem_low, sem_high, axis, at, count):
+        @pl.when(at > 0)
+        def _():
+            pl.semaphore_signal(sem_low, inc=1, device_id={axis: at - 1}, device_id_type=MESH)
+
+        @pl.when(at < count - 1)
+        def _():
+            pl.semaphore_signal(sem_high, inc=1, device_id={axis: at + 1}, device_id_type=MESH)
+
+    greet(barrier, barrier, "rep", r, nr)
+    greet(barrier, barrier, "wide", z, nw)
 
     col_in, movie_in, row_in, gain_in, dil_in, temp_in, mask_in, sup_in, own_in = [
         pltpu.make_async_copy(src, dst, in_s.at[n]) for n, (src, dst) in enumerate((
@@ -116,8 +118,8 @@
         turned = pltpu.roll(kern, (total + 1 + t) % wide_lags, 1, stride=1, stride_axis=0)
         lag_own[t : t + TILE, :] = turned[:, :total].astype(BF)
 
-    pl.semaphore_wait(
-        barrier, nw - 1 + np_ - 1 + (r > 0).astype(I32) + (r < nr - 1).astype(I32))
+    beside = sum((at > 0).astype(I32) + (at < count - 1).astype(I32) for at, count in ((r, nr), (z, nw)))
+    pl.semaphore_wait(barrier, np_ - 1 + beside)
 
     def halo_down(ext, send, recv):
         return pltpu.make_async_remote_copy(
@@ -153,35 +155,68 @@
 
     halo_start(smooth, h1_s, h1_r)
 
-    def to_wide(src, dst, send, recv, k):
+    def vouch(d):
+        greet(far_s.at[1, d], far_s.at[0, d], "wide", z, nw)
+
+    def vouched(d):
+        @pl.when(z > 0)
+        def _():
+            pl.semaphore_wait(far_s.at[0, d], 1)
+
+        @pl.when(z < nw - 1)
+        def _():
+            pl.semaphore_wait(far_s.at[1, d], 1)
+
+    rounds = nw - 2
+    if rounds > 0:
+        vouch(0)
+
+    paired = nw & (nw - 1) == 0
+
+    def peer(k, sign=1):
+        if not paired:
+            return lax.rem(z + nw + sign * k, nw)
+        found, bit = 0, 1
+        while bit < nw:
+            found = found + bit * lax.rem(lax.div(z, bit) + lax.div(k, bit), 2)
+            bit *= 2
+        return found
+
+    def to_wide(src, dst, send, recv, k, slot):
         return pltpu.make_async_remote_copy(
-            src_ref=src, dst_ref=dst, send_sem=send.at[k - 1], recv_sem=recv.at[k - 1],
-            device_id={"wide": lax.rem(z + k, nw)}, device_id_type=MESH)
-
-    def to_plane(src, dst, send, recv, dp, zi):
-        slot = (dp - 1) * nw + zi
+            src_ref=src, dst_ref=dst, send_sem=send.at[slot], recv_sem=recv.at[slot],
+            device_id={"wide": peer(k)}, device_id_type=MESH)
+
+    def to_plane(src, dst, send, recv, dp, slot):
         return pltpu.make_async_remote_copy(
             src_ref=src, dst_ref=dst, send_sem=send.at[slot], recv_sem=recv.at[slot],
             device_id={"planes": lax.rem(p + dp, np_)}, device_id_type=MESH)
 
+    groups = x1_s.shape[0] // ((np_ - 1) * nw)
+    hg = hb // groups
+
+    def some(g):
+        return pl.ds(g * hg, hg)
+
     def lag_copy(k):
-        return to_wide(lag_own, lag_all.at[z], lag_s, lag_r, k)
-
-    def x1_copy(dp, zi):
-        return to_plane(part.at[lax.rem(p + dp, np_) * nw + zi], xrecv.at[(dp - 1) * nw + zi], x1_s, x1_r, dp, zi)
-
-    def z1_copy(k):
-        return to_wide(zsend.at[lax.rem(z + k, nw)], gath.at[z], z1_s, z1_r, k)
-
-    def z2_copy(k):
-        return to_wide(tbuf.at[lax.rem(z + k, nw)], tr_all.at[p * nw + z], z2_s, z2_r, k)
-
-    def x2_copy(dp, zi):
-        return to_plane(tr_all.at[p * nw + zi], tr_all.at[p * nw + zi], x2_s, x2_r, dp, zi)
-
-    for k in range(1, nw):
-        lag_copy(k).start()
-    lag_all[z] = lag_own[...]
+        return to_wide(lag_own, lag_all.at[z], lag_s, lag_r, k, k - 1)
+
+    def x1_copy(dp, zi, g):
+        slot = (dp - 1) * nw + zi
+        return to_plane(
+            part.at[lax.rem(p + dp, np_) * nw + zi, some(g)], xrecv.at[slot, some(g)],
+            x1_s, x1_r, dp, slot * groups + g)
+
+    def z1_copy(k, g):
+        return to_wide(zsend.at[peer(k), some(g)], gath.at[z, some(g)], z1_s, z1_r, k, (k - 1) * groups + g)
+
+    def z2_copy(k, g):
+        return to_wide(
+            tbuf.at[peer(k), some(g)], tr_all.at[p * nw + z, some(g)], z2_s, z2_r, k, (k - 1) * groups + g)
+
+    def x2_copy(dp, zi, g):
+        ours = tr_all.at[p * nw + zi, some(g)]
+        return to_plane(ours, ours, x2_s, x2_r, dp, ((dp - 1) * nw + zi) * groups + g)
 
     temp_in.wait()
     temp32[...] = temp_raw[...].astype(F32)
@@ -195,21 +230,25 @@
         copy.wait()
     mask = mask_ref[...].astype(F32)
     halo_wait(smooth, h1_s, h1_r)
+    if rounds > 0:
+        vouched(0)
+    if rounds > 1:
+        vouch(1)
     for f in range(frames):
         along = jnp.dot(row_fwd[...], smooth[f], preferred_element_type=F32)
         for q in range(planes):
             one = along[:, q * cols : (q + 1) * cols] * mask
             fbuf[q, pl.ds(f, rows, stride=frames), :] = one.astype(BF).astype(F32)
 
-    def project(b):
-        base = pl.multiple_of(b * hb, hb)
-        lines = pl.ds(pl.multiple_of(b * hb * frames, hb * frames), hb * frames)
+    def project(b, g):
+        base = pl.multiple_of(b * hb + g * hg, hg)
+        lines = pl.ds(pl.multiple_of((b * hb + g * hg) * frames, hg * frames), hg * frames)
         x = jnp.concatenate([fbuf[q, lines, :].astype(BF) for q in range(planes)], axis=1)
         pall[...] = jnp.dot(x, temp_t[...], preferred_element_type=F32)
-        sup = sup_ref[pl.ds(base, hb), :]
+        sup = sup_ref[pl.ds(base, hg), :]
         low = lax.rem(sup, LANES)
         high = lax.div(sup, LANES)
-        for i in range(hb):
+        for i in range(hg):
             lo = jnp.broadcast_to(low[i : i + 1, :], (frames, comps))
             hi = jnp.broadcast_to(high[i : i + 1, :], (frames, comps))
             got = jnp.zeros((frames, comps), F32)
@@ -217,34 +256,45 @@
                 piece = pall[i * frames : (i + 1) * frames, q * LANES : (q + 1) * LANES]
                 picked = jnp.take_along_axis(piece, lo, axis=1, mode="promise_in_bounds")
                 got = jnp.where(hi == q, picked, got)
-            part[b, i] = got.astype(BF)
+            part[b, g * hg + i] = got.astype(BF)
 
     def others(n, carry):
-        dp = n // nw + 1
-        zi = lax.rem(z + 1 + lax.rem(n, nw), nw)
-        project(lax.rem(p + dp, np_) * nw + zi)
-        x1_copy(dp, zi).start()
-        return carry
-
-    lax.fori_loop(0, (np_ - 1) * nw, others, 0)
+        g = lax.div(n, (np_ - 1) * nw)
+        dp = lax.rem(lax.div(n, nw), np_ - 1) + 1
+        zi = peer(nw - 1 - lax.rem(n, nw))
+        project(lax.rem(p + dp, np_) * nw + zi, g)
+        x1_copy(dp, zi, g).start()
+        return carry
+
+    lax.fori_loop(0, groups * (np_ - 1) * nw, others, 0)
+
+    for d in range(1, rounds):
+        vouched(d)
+        if d + 1 < rounds:
+            vouch(d + 1)
+    for k in range(1, nw):
+        lag_copy(k).start()
+    lag_all[z] = lag_own[...]
 
     def mine(n, carry):
-        zi = lax.rem(z + 1 + n, nw)
+        g = lax.div(n, nw)
+        k = nw - 1 - lax.rem(n, nw)
+        zi = peer(k)
         b = p * nw + zi
-        project(b)
-        acc = part[b].astype(F32)
+        project(b, g)
+        acc = part[b, some(g)].astype(F32)
         for dp in range(1, np_):
-            x1_copy(dp, zi).wait_recv()
-            acc = acc + xrecv[(dp - 1) * nw + zi].astype(F32)
-        zsend[zi] = acc.astype(BF)
-
-        @pl.when(n < nw - 1)
-        def _():
-            z1_copy(n + 1).start()
-
-        return carry
-
-    lax.fori_loop(0, nw, mine, 0)
+            x1_copy(dp, zi, g).wait_recv()
+            acc = acc + xrecv[(dp - 1) * nw + zi, some(g)].astype(F32)
+        zsend[zi, some(g)] = acc.astype(BF)
+
+        @pl.when(k > 0)
+        def _():
+            z1_copy(lax.max(k, 1), g).start()
+
+        return carry
+
+    lax.fori_loop(0, groups * nw, mine, 0)
     gath[z] = zsend[z]
 
     row_adj[...] = from_taps(row_ref, rim - edge)
@@ -253,37 +303,47 @@
         side = slice(q * cols, (q + 1) * cols)
         col_adj[side, side] = adj_block
 
-    def arrived(k, carry):
+    def tables(k, carry):
         lag_copy(k).wait()
-        z1_copy(k).wait()
-        return carry
-
-    lax.fori_loop(1, nw, arrived, 0)
+        return carry
+
+    lax.fori_loop(1, nw, tables, 0)
+
+    def second(n):
+        return jnp.where(n < 2, n, nw + 1 - n)
 
     me = p * nw + z
-    for i in range(hb):
-        table = lag_all[own_ref[me * hb + i]]
-        columns = gath[:, i].reshape(total, comps)
-        scores = jnp.dot(table, columns, preferred_element_type=F32)
-        tbuf[:, i] = jnp.maximum(scores, 0.0).astype(BF).reshape(nw, frames, comps)
-
-    def give(k, carry):
-        z2_copy(k).start()
-        return carry
-
-    lax.fori_loop(1, nw, give, 0)
-    tr_all[me] = tbuf[z]
+    for g in range(groups):
+        def arrived(k, carry):
+            z1_copy(k, g).wait()
+            return carry
+
+        lax.fori_loop(1, nw, arrived, 0)
+        for i in range(g * hg, (g + 1) * hg):
+            table = lag_all[own_ref[me * hb + i]]
+            columns = gath[:, i].reshape(total, comps)
+            scores = jnp.dot(table, columns, preferred_element_type=F32)
+            tbuf[:, i] = jnp.maximum(scores, 0.0).astype(BF).reshape(nw, frames, comps)
+
+        def give(n, carry):
+            z2_copy(second(n), g).start()
+            return carry
+
+        lax.fori_loop(1, nw, give, 0)
+        tr_all[me, some(g)] = tbuf[z, some(g)]
+        for dp in range(1, np_):
+            x2_copy(dp, z, g).start()
 
     tile = min(256, shapes)
-    groups = tile // TILE
-    ids = (iota((groups, TILE, comps), 0) * TILE + iota((groups, TILE, comps), 1)).astype(F32).astype(BF)
-
-    def model(b):
-        base = pl.multiple_of(b * hb, hb)
-        first = pl.multiple_of(b * hb * frames, hb * frames)
-        sup = sup_ref[pl.ds(base, hb), :]
-        for i in range(hb):
-            now = tr_all[b, i]
+    ids = iota((tile // TILE, TILE, comps), 0) * TILE + iota((tile // TILE, TILE, comps), 1)
+    ids = ids.astype(F32).astype(BF)
+
+    def model(b, g):
+        base = pl.multiple_of(b * hb + g * hg, hg)
+        first = pl.multiple_of((b * hb + g * hg) * frames, hg * frames)
+        sup = sup_ref[pl.ds(base, hg), :]
+        for i in range(hg):
+            now = tr_all[b, g * hg + i]
             tr32[pl.ds(first + i * frames, frames), :] = now.astype(F32)
             for q in range(0, shapes, tile):
                 row = (sup[i : i + 1, :] - q).astype(F32)
@@ -292,32 +352,35 @@
                 fold[i * frames : (i + 1) * frames, q : q + tile] = lax.dot_general(
                     now, hot, (((1,), (1,)), ((), ())), preferred_element_type=F32).astype(BF)
         out = jnp.dot(fold[...], temp[...], preferred_element_type=F32)
-        lines = pl.ds(first, hb * frames)
+        lines = pl.ds(first, hg * frames)
         for q in range(planes):
             fbuf[q, lines, :] = fbuf[q, lines, :] - out[:, q * cols : (q + 1) * cols]
 
-    def same_plane(k, carry):
-        zi = lax.rem(z + nw - k, nw)
+    def same_plane(n, carry):
+        g = lax.div(n, nw)
+        k = second(lax.rem(n, nw))
+        zi = peer(k, -1)
 
         @pl.when(k > 0)
         def _():
-            z2_copy(lax.max(k, 1)).wait_recv()
-
-        for dp in range(1, np_):
-            x2_copy(dp, zi).start()
-        model(p * nw + zi)
-        return carry
-
-    lax.fori_loop(0, nw, same_plane, 0)
+            z2_copy(lax.max(k, 1), g).wait_recv()
+            for dp in range(1, np_):
+                x2_copy(dp, zi, g).start()
+
+        model(p * nw + zi, g)
+        return carry
+
+    lax.fori_loop(0, groups * nw, same_plane, 0)
 
     def other_planes(n, carry):
-        dp = n // nw + 1
-        zi = lax.rem(z + nw - lax.rem(n, nw), nw)
-        x2_copy(dp, zi).wait_recv()
-        model(lax.rem(p + np_ - dp, np_) * nw + zi)
-        return carry
-
-    lax.fori_loop(0, (np_ - 1) * nw, other_planes, 0)
+        g = lax.div(n, (np_ - 1) * nw)
+        dp = lax.rem(lax.div(n, nw), np_ - 1) + 1
+        zi = peer(second(lax.rem(n, nw)), -1)
+        x2_copy(dp, zi, g).wait_recv()
+        model(lax.rem(p + np_ - dp, np_) * nw + zi, g)
+        return carry
+
+    lax.fori_loop(0, groups * (np_ - 1) * nw, other_planes, 0)
 
     for f in range(frames):
         for q in range(planes):
@@ -337,17 +400,18 @@
     halo_wait(resid, h2_s, h2_r)
 
     def drained_planes(n, carry):
-        x1_copy(n // nw + 1, lax.rem(n, nw)).wait_send()
-        x2_copy(n // nw + 1, lax.rem(n, nw)).wait_send()
-        return carry
-
-    lax.fori_loop(0, (np_ - 1) * nw, drained_planes, 0)
-
-    def drained_wide(k, carry):
-        z2_copy(k).wait_send()
-        return carry
-
-    lax.fori_loop(1, nw, drained_wide, 0)
+        dp, zi, g = lax.div(n, nw * groups) + 1, lax.rem(lax.div(n, groups), nw), lax.rem(n, groups)
+        x1_copy(dp, zi, g).wait_send()
+        x2_copy(dp, zi, g).wait_send()
+        return carry
+
+    lax.fori_loop(0, (np_ - 1) * nw * groups, drained_planes, 0)
+
+    def drained_wide(n, carry):
+        z2_copy(lax.div(n, groups) + 1, lax.rem(n, groups)).wait_send()
+        return carry
+
+    lax.fori_loop(0, (nw - 1) * groups, drained_wide, 0)
 
 
 def back_kernel(tr_ref, resid, row_adj, col_adj, tr_hbm, back_hbm, back_out, out_s):
@@ -379,6 +443,7 @@
     nw = lax.axis_size("wide")
     blocks = np_ * nw
     hb = rows // blocks
+    groups = 2 if hb % 2 == 0 else 1
     comps = support.shape[1]
     shapes = templates.shape[0]
     total = nw * frames
@@ -418,7 +483,7 @@
             pltpu.VMEM((total, total), BF),
             pltpu.VMEM((frames, rows + 2 * pad, pixels), BF),
             pltpu.VMEM((planes, rows * frames, cols), F32),
-            pltpu.VMEM((hb * frames, shapes), F32),
+            pltpu.VMEM((hb // groups * frames, shapes), F32),
             pltpu.VMEM((blocks,) + piece, BF),
             pltpu.VMEM(((np_ - 1) * nw,) + piece, BF),
             pltpu.VMEM((nw,) + piece, BF),
@@ -428,13 +493,13 @@
             pltpu.VMEM((blocks,) + piece, BF),
             pltpu.VMEM((rows * frames, comps), F32),
             pltpu.VMEM((share * frames, rows), F32),
-            pltpu.VMEM((hb * frames, shapes), BF),
-            dma((9,)), dma((2,)), dma((2,)), dma((2,)), dma((2,)),
+            pltpu.VMEM((hb // groups * frames, shapes), BF),
+            dma((9,)), pltpu.SemaphoreType.REGULAR((2, max(1, nw - 2))), dma((2,)), dma((2,)), dma((2,)), dma((2,)),
             dma((nw - 1,)), dma((nw - 1,)),
-            dma(((np_ - 1) * nw,)), dma(((np_ - 1) * nw,)),
-            dma((nw - 1,)), dma((nw - 1,)),
-            dma((nw - 1,)), dma((nw - 1,)),
-            dma(((np_ - 1) * nw,)), dma(((np_ - 1) * nw,)),
+            dma(((np_ - 1) * nw * groups,)), dma(((np_ - 1) * nw * groups,)),
+            dma(((nw - 1) * groups,)), dma(((nw - 1) * groups,)),
+            dma(((nw - 1) * groups,)), dma(((nw - 1) * groups,)),
+            dma(((np_ - 1) * nw * groups,)), dma(((np_ - 1) * nw * groups,)),
         ],
         compiler_params=pltpu.CompilerParams(
             collective_id=0, has_side_effects=True, vmem_limit_bytes=40 * 1024 * 1024

time: 35 us -> 35.5 us (1.014)
  Pallas kernels: 34.1 us -> 34.6 us
    pallas_call x1, Pallas kernels: 32.5 us -> 33.1 us  [on_device(): pl.pallas_call(whole_kernel, out_shape=(jax.ShapeDtypeStruct((share, fram...]
where the time goes in v3:
time: 35.5 us; the launch traced here: 35.2 us
  Pallas kernels  34.6 us (97%)
  between operations  0.64 us (2%)
    pallas_call x1, Pallas kernels, on_device(): pl.pallas_call(whole_kernel, out_shape=(jax.ShapeDtypeStruct((share, fram...  33.1 us
    pallas_call x1, Pallas kernels, on_device(): pl.pallas_call(back_kernel, out_shape=(jax.ShapeDtypeStruct((share, frame...  1.55 us

profile of v3, /device:TPU:1, one launch (start us, length us, event | category | flops | bytes accessed | tf_op | source)
XLA Modules:
  0.0 35.2 jit_solution(9240064793806222764)
XLA Ops:
  0.6 33.1 %shard_map.104 = (bf16[64,16,128]{2,1,0:T(8,128)(2,1)S(1)}, bf16[16,160,256]{2,1,0:T(8,128)(2,1)S(1)}, bf16[128,160]{1,0:T(8,128)(2,1)S(1)}, bf16[256,256]{1,0:T(8,128)(2,1)S(1)}) custom-call(bf16[2,16,128,128]{3,2,1,0:T(8,128)(2,1)} %movie_hbm.1, bf16[1024,128]{1,0:T(8,128)(2,1)} %bitcast.4, s32[128,128]{1,0:T(8,128)} %sup_hbm.1, s32[128,128]{1,0:T(8,128)} %mask_hbm.1, ...), custom_call_target="tpu_custom_call" | custom-call | tf_op jit(solution)/shard_map/pallas_call | solution.py:458
  33.7 1.5 %shard_map.105 = (bf16[64,16,128]{2,1,0:T(8,128)(2,1)}, bf16[2,16,128,128]{3,2,1,0:T(8,128)(2,1)}) custom-call(bf16[64,16,128]{2,1,0:T(8,128)(2,1)S(1)} %get-tuple-element.6.tr_ref, bf16[16,160,256]{2,1,0:T(8,128)(2,1)S(1)} %get-tuple-element.7.resid, bf16[128,160]{1,0:T(8,128)(2,1)S(1)} %get-tuple-element.8.row_adj, ...), custom_call_target="tpu_custom_call" | custom-call | tf_op jit(solution)/shard_map/pallas_call | solution.py:511

commit v4 on v3

--- a/solution.py
+++ b/solution.py
@@ -171,7 +171,7 @@
     if rounds > 0:
         vouch(0)
 
-    paired = nw & (nw - 1) == 0
+    paired = False
 
     def peer(k, sign=1):
         if not paired:
@@ -443,7 +443,7 @@
     nw = lax.axis_size("wide")
     blocks = np_ * nw
     hb = rows // blocks
-    groups = 2 if hb % 2 == 0 else 1
+    groups = 1
     comps = support.shape[1]
     shapes = templates.shape[0]
     total = nw * frames

time: 35.5 us -> 34.3 us (0.966)
  Pallas kernels: 34.6 us -> 33.4 us
    pallas_call x1, Pallas kernels: 33.1 us -> 31.8 us  [on_device(): pl.pallas_call(whole_kernel, out_shape=(jax.ShapeDtypeStruct((share, fram...]
where the time goes in v4:
time: 34.3 us; the launch traced here: 34 us
  Pallas kernels  33.4 us (97%)
  between operations  0.64 us (2%)
    pallas_call x1, Pallas kernels, on_device(): pl.pallas_call(whole_kernel, out_shape=(jax.ShapeDtypeStruct((share, fram...  31.8 us
    pallas_call x1, Pallas kernels, on_device(): pl.pallas_call(back_kernel, out_shape=(jax.ShapeDtypeStruct((share, frame...  1.55 us

profile of v4, /device:TPU:1, one launch (start us, length us, event | category | flops | bytes accessed | tf_op | source)
XLA Modules:
  0.0 34.0 jit_solution(5570693653624174868)
XLA Ops:
  0.6 31.8 %shard_map.104 = (bf16[64,16,128]{2,1,0:T(8,128)(2,1)S(1)}, bf16[16,160,256]{2,1,0:T(8,128)(2,1)S(1)}, bf16[128,160]{1,0:T(8,128)(2,1)S(1)}, bf16[256,256]{1,0:T(8,128)(2,1)S(1)}) custom-call(bf16[2,16,128,128]{3,2,1,0:T(8,128)(2,1)} %movie_hbm.1, bf16[1024,128]{1,0:T(8,128)(2,1)} %bitcast.4, s32[128,128]{1,0:T(8,128)} %sup_hbm.1, s32[128,128]{1,0:T(8,128)} %mask_hbm.1, ...), custom_call_target="tpu_custom_call" | custom-call | tf_op jit(solution)/shard_map/pallas_call | solution.py:458
  32.5 1.5 %shard_map.105 = (bf16[64,16,128]{2,1,0:T(8,128)(2,1)}, bf16[2,16,128,128]{3,2,1,0:T(8,128)(2,1)}) custom-call(bf16[64,16,128]{2,1,0:T(8,128)(2,1)S(1)} %get-tuple-element.6.tr_ref, bf16[16,160,256]{2,1,0:T(8,128)(2,1)S(1)} %get-tuple-element.7.resid, bf16[128,160]{1,0:T(8,128)(2,1)S(1)} %get-tuple-element.8.row_adj, ...), custom_call_target="tpu_custom_call" | custom-call | tf_op jit(solution)/shard_map/pallas_call | solution.py:511
